TPU v7x, 32 devices: a whole 2x2x4 slice. The times are simulated.
32 devices in a mesh: slab: 8 (over z, y), sub: 4 (over x, core).
Axes of the slice: x: 2, y: 2, z: 4, core: 2. Of those that a mesh axis runs over, the one named last changes fastest.
Arguments:
- start: float32 [64, 6, 2, 16, 128], P(('slab', 'sub')), may hold values from -20 to 20
- inv_factor: bfloat16 [1024, 2, 128, 128], P(('slab', 'sub')), as said below
- partner: int32 [64, 6], P(('slab', 'sub')), may hold values from -1 to 63, as said below
- partner_face: int32 [64, 6], P(('slab', 'sub')), may hold values from -1 to 5, as said below
- elem_class: int32 [64, 16], P(('slab', 'sub')), may hold values from 0 to 3
- elem_face: int32 [64, 16], P(('slab', 'sub')), may hold values from 0 to 5
- load_map: bfloat16 [4, 2, 128, 128], replicated, may hold values from -0.375 to 0.375
- trace_map: bfloat16 [4, 2, 128, 128], replicated, may hold values from -0.25 to 0.25
Outputs:
- last_block: float32 [64, 6, 2, 16, 128], P(('slab', 'sub'))
- hessenberg: float32 [4, 5, 16, 16], replicated
Inputs may be any that keep to these rules, and one draw needn't show every extreme that they name: Global subdomain s lies on device s // 2 of the joined axes. Across faces 0 and 1 the partner lies on the same device; across face 2 on the device one lower along sub, face 3 one higher along sub, face 4 one lower along slab, face 5 one higher along slab, and -1 exactly where no such device exists. `partner_face`: faces 0 and 1 meet face 0 or 1 of their partner; faces 2, 3, 4, 5 meet faces 3, 2, 5, 4; -1 exactly where partner is -1. `inv_factor`: each factor is lower triangular with a real diagonal of 0.5 to 2 and a small imaginary diagonal.
All inputs are finite; a program needn't handle non-finite values.
Results may differ from a plain program's by a relative error of at most 0.013.
Values sent between devices are 32-bit elements; how exact they have to be, the bound alone decides.
No kernel may reach another device: no remote copies, remote signals or barrier semaphores. Data moves between devices by JAX's collectives and lax.ppermute only.
A program may use at most 64 MiB of HBM per device.

v0:
```python
import jax
import jax.numpy as jnp
from jax import lax
from jax.sharding import PartitionSpec as P

ITERS = 4
HIGHEST_PRECISION = lax.Precision.HIGHEST


def extended(x, sides, width):
    for axis, dim in sides:
        count, length = (lax.axis_size(axis), x.shape[dim])
        up = [(i, (i + 1) % count) for i in range(count - 1)]
        down = [(j, i) for i, j in up]
        last = lax.slice_in_dim(x, length - width, length, axis=dim)
        leading = lax.slice_in_dim(x, 0, width, axis=dim)
        before = lax.ppermute(last, axis, up)
        after = lax.ppermute(leading, axis, down)
        x = jnp.concatenate([before, x, after], axis=dim)
    return x


def complex_apply(layout, matrix_real, matrix_imag, vec_real, vec_imag):
    real_part = jnp.einsum(
        layout, matrix_real, vec_real, preferred_element_type=jnp.float32
    ) - jnp.einsum(layout, matrix_imag, vec_imag, preferred_element_type=jnp.float32)
    imag_part = jnp.einsum(
        layout, matrix_real, vec_imag, preferred_element_type=jnp.float32
    ) + jnp.einsum(layout, matrix_imag, vec_real, preferred_element_type=jnp.float32)
    return (real_part, imag_part)


def factor_apply(inv_factor, vector_b, adjoint):
    factor_real = inv_factor[:, 0]
    factor_imag = inv_factor[:, 1]
    vec_real = vector_b[:, 0]
    vec_imag = vector_b[:, 1]
    if adjoint:
        layout = "eji,erj->eri"
        real_part = jnp.einsum(
            layout, factor_real, vec_real, preferred_element_type=jnp.float32
        ) + jnp.einsum(layout, factor_imag, vec_imag, preferred_element_type=jnp.float32)
        imag_part = jnp.einsum(
            layout, factor_real, vec_imag, preferred_element_type=jnp.float32
        ) - jnp.einsum(layout, factor_imag, vec_real, preferred_element_type=jnp.float32)
    else:
        layout = "eij,erj->eri"
        real_part, imag_part = complex_apply(layout, factor_real, factor_imag, vec_real, vec_imag)
    return jnp.stack([real_part, imag_part], axis=1)


def partner_traces(outgoing, partner, partner_face):
    sub_count = outgoing.shape[0]
    has_partner = partner >= 0
    local_index = jnp.where(has_partner, partner % sub_count, 0)
    face_index = jnp.where(has_partner, partner_face, 0)
    beside_all = extended(outgoing[None, None], (("slab", 0), ("sub", 1)), 1)
    trace_pool = beside_all.reshape((9 * sub_count * 6,) + outgoing.shape[2:])
    block_table = jnp.array([4, 4, 3, 5, 1, 7], jnp.int32)
    source_slot = (block_table[None, :] * sub_count + local_index) * 6 + face_index
    picked = trace_pool[source_slot]
    return jnp.where(has_partner[:, :, None, None, None], picked, 0.0)


def apply_operator(
    vector, inv_factor, partner, partner_face, elem_class, elem_face, load_map, trace_map
):
    sub_count = vector.shape[0]
    elem_count = elem_class.shape[1]
    rhs_count = vector.shape[3]
    wave_count = load_map.shape[2]
    vector_b = vector.astype(jnp.bfloat16)
    elem_load_map = load_map[elem_class]
    elem_trace_map = trace_map[elem_class]
    face_traces = jnp.take_along_axis(vector_b, elem_face[:, :, None, None, None], axis=1)
    load_real, load_imag = complex_apply(
        "sepq,serq->serp",
        elem_load_map[:, :, 0],
        elem_load_map[:, :, 1],
        face_traces[:, :, 0],
        face_traces[:, :, 1],
    )
    chosen_b = (
        jnp.stack([load_real, load_imag], axis=2)
        .astype(jnp.bfloat16)
        .reshape(sub_count * elem_count, 2, rhs_count, wave_count)
    )
    middle = factor_apply(inv_factor, chosen_b, False).astype(jnp.bfloat16)
    coefficients = (
        factor_apply(inv_factor, middle, True)
        .astype(jnp.bfloat16)
        .reshape(sub_count, elem_count, 2, rhs_count, wave_count)
    )
    trace_real, trace_imag = complex_apply(
        "seqp,serp->serq",
        elem_trace_map[:, :, 0],
        elem_trace_map[:, :, 1],
        coefficients[:, :, 0],
        coefficients[:, :, 1],
    )
    accumulated = jnp.stack([trace_real, trace_imag], axis=2)
    face_onehot = (elem_face[:, :, None] == jnp.arange(6, dtype=jnp.int32)[None, None, :]).astype(
        jnp.float32
    )
    outgoing = (
        jnp.einsum("sef,sexrq->sfxrq", face_onehot, accumulated, precision=HIGHEST_PRECISION)
        - vector
    )
    return vector - partner_traces(outgoing, partner, partner_face)


def local_inner(left, right):
    return jnp.einsum("sfxiq,sfxjq->ij", left, right, precision=HIGHEST_PRECISION)


def normalize(vector, gram_matrix):
    low_factor = jnp.linalg.cholesky(gram_matrix)
    identity = jnp.eye(gram_matrix.shape[0], dtype=jnp.float32)
    inverse = lax.linalg.triangular_solve(low_factor, identity, left_side=True, lower=True)
    return (
        jnp.einsum("sfxaq,ba->sfxbq", vector, inverse, precision=HIGHEST_PRECISION),
        low_factor.T,
    )


def body(start, inv_factor, partner, partner_face, elem_class, elem_face, load_map, trace_map):
    rhs_count = start.shape[3]
    entry_count = start.size // rhs_count * lax.axis_size("slab") * lax.axis_size("sub")
    start_gram = lax.psum(local_inner(start, start), ("slab", "sub")) / entry_count
    basis_block, upper_factor = normalize(start, start_gram)
    blocks = [basis_block]
    hessenberg = jnp.zeros((ITERS, ITERS + 1, rhs_count, rhs_count), jnp.float32)
    for number in range(ITERS):
        image_block = apply_operator(
            blocks[-1],
            inv_factor,
            partner,
            partner_face,
            elem_class,
            elem_face,
            load_map,
            trace_map,
        )
        stacked = jnp.stack(blocks)
        local_terms = jnp.einsum(
            "ksfxiq,sfxjq->kij", stacked, image_block, precision=HIGHEST_PRECISION
        )
        summed_terms, raw_gram = lax.psum(
            (local_terms, local_inner(image_block, image_block)), ("slab", "sub")
        )
        projection = summed_terms / entry_count
        image_block = image_block - jnp.einsum(
            "ksfxaq,kab->sfxbq", stacked, projection, precision=HIGHEST_PRECISION
        )
        gram_matrix = raw_gram / entry_count - jnp.einsum(
            "kai,kaj->ij", projection, projection, precision=HIGHEST_PRECISION
        )
        basis_block, upper_factor = normalize(image_block, gram_matrix)
        hessenberg = hessenberg.at[number, : number + 1].set(projection)
        hessenberg = hessenberg.at[number, number + 1].set(upper_factor)
        blocks.append(basis_block)
    return (blocks[-1], hessenberg)


def solution(mesh):
    placed = (
        P(("slab", "sub"), None, None, None, None),
        P(("slab", "sub"), None, None, None),
        P(("slab", "sub"), None),
        P(("slab", "sub"), None),
        P(("slab", "sub"), None),
        P(("slab", "sub"), None),
        P(),
        P(),
    )
    return jax.shard_map(
        body,
        mesh=mesh,
        in_specs=placed,
        out_specs=(P(("slab", "sub"), None, None, None, None), P()),
        check_vma=False,
    )
```

profile of v0, /device:TPU:0, one launch (start us, length us, event | category | flops | bytes accessed | tf_op | source)
XLA Modules:
  0.0 421.1 jit_solution(14362382191184048011)
XLA Ops:
  2.8 2.1 gather_fusion
  7.2 42.0 %psum.63 = f32[16,16]{0,1:T(8,128)S(1)} all-reduce(f32[16,16]{0,1:T(8,128)S(1)} %convolution_bitcast_fusion.21), channel_id=1, replica_groups=mesh['slab'=8,'sub'=4] {'slab','sub'}, use_global_device_ids=true, to_apply=%region_0.0 | all-reduce | flops 256 | bytes 2048 | tf_op jit(solution)/shard_map/psum | solution.py:129
  55.4 2.0 fusion.119
  57.4 1.9 fusion.13
  59.3 1.9 fusion.12
  65.1 2.1 gather_fusion.1
  73.9 4.8 %collective-permute-start = (f32[1,1,2,6,2,16,128]{6,5,4,3,2,1,0:T(8,128)S(1)}, f32[1,1,2,6,2,16,128]{6,5,4,3,2,1,0:T(8,128)S(1)}, u32[]{:S(2)}, u32[]{:S(2)}) collective-permute-start(f32[1,1,2,6,2,16,128]{6,5,4,3,2,1,0:T(8,128)S(1)} %fusion.108), channel_id=1, source_target_pairs={{0,4},{4,8},{8,12},{12,16},{16,20},{20,24},{24,28},{1,5},{5,9},{9,... | collective-permute-start | bytes 589832 | tf_op jit(solution)/shard_map/ppermute | solution.py:17
  80.4 3.9 collective-permute-done
  86.4 3.9 collective-permute-start.2
  91.4 2.7 pad_maximum_fusion
  94.2 2.0 gather_fusion.2
  97.0 48.7 %all-reduce.4 = (f32[16,16]{0,1:T(8,128)S(1)}, f32[1,16,16]{2,1,0:T(8,128)S(1)}) all-reduce(f32[16,16]{0,1:T(8,128)S(1)} %convolution_bitcast_fusion.20, f32[1,16,16]{2,1,0:T(8,128)S(1)} %convolution_bitcast_fusion.19), channel_id=1, replica_groups=mesh['slab'=8,'sub'=4] {'slab','sub'}, use_global_device_ids=true, to_apply=%region_3.7 | all-reduce | flops 512 | bytes 4096 | tf_op jit(solution)/shard_map/psum | solution.py:148
  152.2 2.0 fusion.116
  154.2 1.9 fusion.117
  166.3 4.8 %collective-permute-start.4 = (f32[1,1,2,6,2,16,128]{6,5,4,3,2,1,0:T(8,128)S(1)}, f32[1,1,2,6,2,16,128]{6,5,4,3,2,1,0:T(8,128)S(1)}, u32[]{:S(2)}, u32[]{:S(2)}) collective-permute-start(f32[1,1,2,6,2,16,128]{6,5,4,3,2,1,0:T(8,128)S(1)} %fusion.103), channel_id=1, source_target_pairs={{0,4},{4,8},{8,12},{12,16},{16,20},{20,24},{24,28},{1,5},{5,9},{9,... | collective-permute-start | bytes 589832 | tf_op jit(solution)/shard_map/ppermute | solution.py:17
  172.9 3.8 collective-permute-done.4
  178.1 3.1 collective-permute-start.6
  184.1 2.0 gather_fusion.3
  187.1 47.8 %all-reduce.3 = (f32[2,16,16]{2,1,0:T(8,128)S(1)}, f32[16,16]{0,1:T(8,128)S(1)}) all-reduce(f32[2,16,16]{2,1,0:T(8,128)S(1)} %convolution_bitcast_fusion.7, f32[16,16]{0,1:T(8,128)S(1)} %convolution_bitcast_fusion.18), channel_id=1, replica_groups=mesh['slab'=8,'sub'=4] {'slab','sub'}, use_global_device_ids=true, to_apply=%region_6.10 | all-reduce | flops 768 | bytes 6144 | tf_op jit(solution)/shard_map/psum | solution.py:148
  241.4 2.0 fusion.114
  243.4 1.9 fusion.115
  255.5 4.9 %collective-permute-start.8 = (f32[1,1,2,6,2,16,128]{6,5,4,3,2,1,0:T(8,128)S(1)}, f32[1,1,2,6,2,16,128]{6,5,4,3,2,1,0:T(8,128)S(1)}, u32[]{:S(2)}, u32[]{:S(2)}) collective-permute-start(f32[1,1,2,6,2,16,128]{6,5,4,3,2,1,0:T(8,128)S(1)} %fusion.101), channel_id=1, source_target_pairs={{0,4},{4,8},{8,12},{12,16},{16,20},{20,24},{24,28},{1,5},{5,9},{9,... | collective-permute-start | bytes 589832 | tf_op jit(solution)/shard_map/ppermute | solution.py:17
  262.1 3.9 collective-permute-done.8
  267.3 3.1 collective-permute-start.10
  273.3 2.0 gather_fusion.4
  276.5 49.0 %all-reduce.2 = (f32[3,16,16]{2,1,0:T(8,128)S(1)}, f32[16,16]{0,1:T(8,128)S(1)}) all-reduce(f32[3,16,16]{2,1,0:T(8,128)S(1)} %convolution_bitcast_fusion.6, f32[16,16]{0,1:T(8,128)S(1)} %convolution_bitcast_fusion.17), channel_id=1, replica_groups=mesh['slab'=8,'sub'=4] {'slab','sub'}, use_global_device_ids=true, to_apply=%region_8.12 | all-reduce | flops 1024 | bytes 8192 | tf_op jit(solution)/shard_map/psum | solution.py:148
  332.2 2.0 fusion.112
  334.2 1.9 fusion.113
  346.3 4.8 %collective-permute-start.12 = (f32[1,1,2,6,2,16,128]{6,5,4,3,2,1,0:T(8,128)S(1)}, f32[1,1,2,6,2,16,128]{6,5,4,3,2,1,0:T(8,128)S(1)}, u32[]{:S(2)}, u32[]{:S(2)}) collective-permute-start(f32[1,1,2,6,2,16,128]{6,5,4,3,2,1,0:T(8,128)S(1)} %fusion.99), channel_id=1, source_target_pairs={{0,4},{4,8},{8,12},{12,16},{16,20},{20,24},{24,28},{1,5},{5,9},{9,... | collective-permute-start | bytes 589832 | tf_op jit(solution)/shard_map/ppermute | solution.py:17
  352.8 3.7 collective-permute-done.12
  357.9 3.8 collective-permute-start.14
  366.6 47.3 %all-reduce.1 = (f32[4,16,16]{2,1,0:T(8,128)S(1)}, f32[16,16]{0,1:T(8,128)S(1)}) all-reduce(f32[4,16,16]{2,1,0:T(8,128)S(1)} %convolution_bitcast_fusion.5, f32[16,16]{0,1:T(8,128)S(1)} %convolution_bitcast_fusion.16), channel_id=1, replica_groups=mesh['slab'=8,'sub'=4] {'slab','sub'}, use_global_device_ids=true, to_apply=%region_10.14 | all-reduce | flops 1280 | bytes 10240 | tf_op jit(solution)/shard_map/psum | solution.py:148
  (251 shorter events, 106.1 us)
Async XLA Ops:
  6.9 47.9 %copy-start.2 = (bf16[32,2,128,128]{3,2,0,1:T(8,128)(2,1)}, bf16[32,2,128,128]{3,2,0,1:T(8,128)(2,1)S(1)}, u32[]{:S(2)}) copy-start(bf16[32,2,128,128]{3,2,0,1:T(8,128)(2,1)S(1)} %copy.19) | copy-start | bytes 6291460
  55.4 5.8 %copy-start.1 = (bf16[32,2,128,128]{3,2,1,0:T(8,128)(2,1)S(1)}, bf16[32,2,128,128]{3,2,1,0:T(8,128)(2,1)}, u32[]{:S(2)}) copy-start(bf16[32,2,128,128]{3,2,1,0:T(8,128)(2,1)} %param.34) | copy-start | bytes 6291460
  72.0 18.3 %copy-start.24 = (s32[2,6]{1,0:T(2,128)S(1)}, s32[2,6]{1,0:T(2,128)}, u32[]{:S(2)}) copy-start(s32[2,6]{1,0:T(2,128)} %param.36) | copy-start | bytes 148
  72.0 18.3 %copy-start.25 = (s32[2,6]{1,0:T(2,128)S(1)}, s32[2,6]{1,0:T(2,128)}, u32[]{:S(2)}) copy-start(s32[2,6]{1,0:T(2,128)} %param.35) | copy-start | bytes 148
  72.0 18.3 %copy-start.26 = (s32[6]{0:T(128)S(1)}, s32[6]{0:T(128)}, u32[]{:S(2)}) copy-start(s32[6]{0:T(128)} %constant.343) | copy-start | bytes 76
  72.6 7.8 %collective-permute-start.1 = (f32[1,1,2,6,2,16,128]{6,5,4,3,2,1,0:T(8,128)S(1)}, f32[1,1,2,6,2,16,128]{6,5,4,3,2,1,0:T(8,128)S(1)}, u32[]{:S(2)}, u32[]{:S(2)}) collective-permute-start(f32[1,1,2,6,2,16,128]{6,5,4,3,2,1,0:T(8,128)S(1)} %fusion.108), channel_id=1, source_target_pairs={{4,0},{8,4},{12,8},{16,12},{20,16},{24,20},{28,24},{5,1},{9,5},{13... | collective-permute-start | bytes 589832 | tf_op jit(solution)/shard_map/ppermute | solution.py:18
  73.9 10.4 %collective-permute-start = (f32[1,1,2,6,2,16,128]{6,5,4,3,2,1,0:T(8,128)S(1)}, f32[1,1,2,6,2,16,128]{6,5,4,3,2,1,0:T(8,128)S(1)}, u32[]{:S(2)}, u32[]{:S(2)}) collective-permute-start(f32[1,1,2,6,2,16,128]{6,5,4,3,2,1,0:T(8,128)S(1)} %fusion.108), channel_id=1, source_target_pairs={{0,4},{4,8},{8,12},{12,16},{16,20},{20,24},{24,28},{1,5},{5,9},{9,... | collective-permute-start | bytes 589832 | tf_op jit(solution)/shard_map/ppermute | solution.py:17
  85.2 5.3 %collective-permute-start.3 = (f32[3,1,2,6,2,16,128]{6,5,4,3,2,1,0:T(8,128)}, f32[3,1,2,6,2,16,128]{6,5,4,3,2,1,0:T(8,128)}, u32[]{:S(2)}, u32[]{:S(2)}) collective-permute-start(f32[3,1,2,6,2,16,128]{6,5,4,3,2,1,0:T(8,128)} %pad_maximum_fusion.5), channel_id=1, source_target_pairs={{1,0},{2,1},{3,2},{5,4},{6,5},{7,6},{9,8},{10,9},{11,10},{13,12},{... | collective-permute-start | bytes 1769480 | tf_op jit(solution)/shard_map/ppermute | solution.py:18
  86.4 5.0 %collective-permute-start.2 = (f32[3,1,2,6,2,16,128]{6,5,4,3,2,1,0:T(8,128)}, f32[3,1,2,6,2,16,128]{6,5,4,3,2,1,0:T(8,128)}, u32[]{:S(2)}, u32[]{:S(2)}) collective-permute-start(f32[3,1,2,6,2,16,128]{6,5,4,3,2,1,0:T(8,128)} %pad_maximum_fusion.5), channel_id=1, source_target_pairs={{0,1},{1,2},{2,3},{4,5},{5,6},{6,7},{8,9},{9,10},{10,11},{12,13},{... | collective-permute-start | bytes 1769480 | tf_op jit(solution)/shard_map/ppermute | solution.py:17
  90.4 184.9 %copy-start.22 = (pred[2,6]{1,0:T(4,128)(4,1)}, pred[2,6]{1,0:T(4,128)(4,1)S(1)}, u32[]{:S(2)}) copy-start(pred[2,6]{1,0:T(4,128)(4,1)S(1)} %broadcast_compare_fusion) | copy-start | bytes 40
  152.1 4.0 copy-start.3
  165.0 7.9 %collective-permute-start.5 = (f32[1,1,2,6,2,16,128]{6,5,4,3,2,1,0:T(8,128)S(1)}, f32[1,1,2,6,2,16,128]{6,5,4,3,2,1,0:T(8,128)S(1)}, u32[]{:S(2)}, u32[]{:S(2)}) collective-permute-start(f32[1,1,2,6,2,16,128]{6,5,4,3,2,1,0:T(8,128)S(1)} %fusion.103), channel_id=1, source_target_pairs={{4,0},{8,4},{12,8},{16,12},{20,16},{24,20},{28,24},{5,1},{9,5},{13... | collective-permute-start | bytes 589832 | tf_op jit(solution)/shard_map/ppermute | solution.py:18
  166.3 10.4 %collective-permute-start.4 = (f32[1,1,2,6,2,16,128]{6,5,4,3,2,1,0:T(8,128)S(1)}, f32[1,1,2,6,2,16,128]{6,5,4,3,2,1,0:T(8,128)S(1)}, u32[]{:S(2)}, u32[]{:S(2)}) collective-permute-start(f32[1,1,2,6,2,16,128]{6,5,4,3,2,1,0:T(8,128)S(1)} %fusion.103), channel_id=1, source_target_pairs={{0,4},{4,8},{8,12},{12,16},{16,20},{20,24},{24,28},{1,5},{5,9},{9,... | collective-permute-start | bytes 589832 | tf_op jit(solution)/shard_map/ppermute | solution.py:17
  176.8 4.4 %collective-permute-start.7 = (f32[3,1,2,6,2,16,128]{6,5,4,3,2,1,0:T(8,128)S(1)}, f32[3,1,2,6,2,16,128]{6,5,4,3,2,1,0:T(8,128)S(1)}, u32[]{:S(2)}, u32[]{:S(2)}) collective-permute-start(f32[3,1,2,6,2,16,128]{6,5,4,3,2,1,0:T(8,128)S(1)} %pad_maximum_fusion.6), channel_id=1, source_target_pairs={{1,0},{2,1},{3,2},{5,4},{6,5},{7,6},{9,8},{10,9},{11,10},{13,12},{... | collective-permute-start | bytes 1769480 | tf_op jit(solution)/shard_map/ppermute | solution.py:18
  178.1 4.7 %collective-permute-start.6 = (f32[3,1,2,6,2,16,128]{6,5,4,3,2,1,0:T(8,128)S(1)}, f32[3,1,2,6,2,16,128]{6,5,4,3,2,1,0:T(8,128)S(1)}, u32[]{:S(2)}, u32[]{:S(2)}) collective-permute-start(f32[3,1,2,6,2,16,128]{6,5,4,3,2,1,0:T(8,128)S(1)} %pad_maximum_fusion.6), channel_id=1, source_target_pairs={{0,1},{1,2},{2,3},{4,5},{5,6},{6,7},{8,9},{9,10},{10,11},{12,13},{... | collective-permute-start | bytes 1769480 | tf_op jit(solution)/shard_map/ppermute | solution.py:17
  234.8 5.3 %copy-start.16 = (f32[2,16,16]{2,1,0:T(8,128)}, f32[2,16,16]{2,1,0:T(8,128)S(1)}, u32[]{:S(2)}) copy-start(f32[2,16,16]{2,1,0:T(8,128)S(1)} %get-tuple-element.105) | copy-start | bytes 6148
  241.3 4.0 copy-start.4
  254.2 7.9 %collective-permute-start.9 = (f32[1,1,2,6,2,16,128]{6,5,4,3,2,1,0:T(8,128)S(1)}, f32[1,1,2,6,2,16,128]{6,5,4,3,2,1,0:T(8,128)S(1)}, u32[]{:S(2)}, u32[]{:S(2)}) collective-permute-start(f32[1,1,2,6,2,16,128]{6,5,4,3,2,1,0:T(8,128)S(1)} %fusion.101), channel_id=1, source_target_pairs={{4,0},{8,4},{12,8},{16,12},{20,16},{24,20},{28,24},{5,1},{9,5},{13... | collective-permute-start | bytes 589832 | tf_op jit(solution)/shard_map/ppermute | solution.py:18
  255.5 10.4 %collective-permute-start.8 = (f32[1,1,2,6,2,16,128]{6,5,4,3,2,1,0:T(8,128)S(1)}, f32[1,1,2,6,2,16,128]{6,5,4,3,2,1,0:T(8,128)S(1)}, u32[]{:S(2)}, u32[]{:S(2)}) collective-permute-start(f32[1,1,2,6,2,16,128]{6,5,4,3,2,1,0:T(8,128)S(1)} %fusion.101), channel_id=1, source_target_pairs={{0,4},{4,8},{8,12},{12,16},{16,20},{20,24},{24,28},{1,5},{5,9},{9,... | collective-permute-start | bytes 589832 | tf_op jit(solution)/shard_map/ppermute | solution.py:17
  266.0 5.0 %collective-permute-start.11 = (f32[3,1,2,6,2,16,128]{6,5,4,3,2,1,0:T(8,128)S(1)}, f32[3,1,2,6,2,16,128]{6,5,4,3,2,1,0:T(8,128)S(1)}, u32[]{:S(2)}, u32[]{:S(2)}) collective-permute-start(f32[3,1,2,6,2,16,128]{6,5,4,3,2,1,0:T(8,128)S(1)} %pad_maximum_fusion.7), channel_id=1, source_target_pairs={{1,0},{2,1},{3,2},{5,4},{6,5},{7,6},{9,8},{10,9},{11,10},{13,12},{... | collective-permute-start | bytes 1769480 | tf_op jit(solution)/shard_map/ppermute | solution.py:18
  267.3 4.7 %collective-permute-start.10 = (f32[3,1,2,6,2,16,128]{6,5,4,3,2,1,0:T(8,128)S(1)}, f32[3,1,2,6,2,16,128]{6,5,4,3,2,1,0:T(8,128)S(1)}, u32[]{:S(2)}, u32[]{:S(2)}) collective-permute-start(f32[3,1,2,6,2,16,128]{6,5,4,3,2,1,0:T(8,128)S(1)} %pad_maximum_fusion.7), channel_id=1, source_target_pairs={{0,1},{1,2},{2,3},{4,5},{5,6},{6,7},{8,9},{9,10},{10,11},{12,13},{... | collective-permute-start | bytes 1769480 | tf_op jit(solution)/shard_map/ppermute | solution.py:17
  325.5 5.4 %copy-start.14 = (f32[3,16,16]{2,1,0:T(8,128)}, f32[3,16,16]{2,1,0:T(8,128)S(1)}, u32[]{:S(2)}) copy-start(f32[3,16,16]{2,1,0:T(8,128)S(1)} %get-tuple-element.103) | copy-start | bytes 9220
  343.8 7.4 %copy-start.18 = (f32[1,1,16,16]{2,3,1,0:T(8,128)S(1)}, f32[1,1,16,16]{2,3,1,0:T(8,128)}, u32[]{:S(2)}) copy-start(f32[1,1,16,16]{2,3,1,0:T(8,128)} %get-tuple-element.115) | copy-start | bytes 3076
  343.8 8.7 %copy-start.19 = (f32[1,1,16,16]{2,3,1,0:T(8,128)S(1)}, f32[1,1,16,16]{2,3,1,0:T(8,128)}, u32[]{:S(2)}) copy-start(f32[1,1,16,16]{2,3,1,0:T(8,128)} %get-tuple-element.113) | copy-start | bytes 3076
  344.4 17.3 %copy-start.17 = (f32[2,16,16]{2,1,0:T(8,128)S(1)}, f32[2,16,16]{2,1,0:T(8,128)}, u32[]{:S(2)}) copy-start(f32[2,16,16]{2,1,0:T(8,128)} %copy-done.16) | copy-start | bytes 6148
  344.4 17.3 %copy-start.20 = (f32[1,1,16,16]{2,3,1,0:T(8,128)S(1)}, f32[1,1,16,16]{2,3,1,0:T(8,128)}, u32[]{:S(2)}) copy-start(f32[1,1,16,16]{2,3,1,0:T(8,128)} %get-tuple-element.111) | copy-start | bytes 3076
  344.4 17.4 %copy-start.15 = (f32[3,16,16]{2,1,0:T(8,128)S(1)}, f32[3,16,16]{2,1,0:T(8,128)}, u32[]{:S(2)}) copy-start(f32[3,16,16]{2,1,0:T(8,128)} %copy-done.14) | copy-start | bytes 9220
  345.0 7.8 %collective-permute-start.13 = (f32[1,1,2,6,2,16,128]{6,5,4,3,2,1,0:T(8,128)S(1)}, f32[1,1,2,6,2,16,128]{6,5,4,3,2,1,0:T(8,128)S(1)}, u32[]{:S(2)}, u32[]{:S(2)}) collective-permute-start(f32[1,1,2,6,2,16,128]{6,5,4,3,2,1,0:T(8,128)S(1)} %fusion.99), channel_id=1, source_target_pairs={{4,0},{8,4},{12,8},{16,12},{20,16},{24,20},{28,24},{5,1},{9,5},{13... | collective-permute-start | bytes 589832 | tf_op jit(solution)/shard_map/ppermute | solution.py:18
  346.3 10.2 %collective-permute-start.12 = (f32[1,1,2,6,2,16,128]{6,5,4,3,2,1,0:T(8,128)S(1)}, f32[1,1,2,6,2,16,128]{6,5,4,3,2,1,0:T(8,128)S(1)}, u32[]{:S(2)}, u32[]{:S(2)}) collective-permute-start(f32[1,1,2,6,2,16,128]{6,5,4,3,2,1,0:T(8,128)S(1)} %fusion.99), channel_id=1, source_target_pairs={{0,4},{4,8},{8,12},{12,16},{16,20},{20,24},{24,28},{1,5},{5,9},{9,... | collective-permute-start | bytes 589832 | tf_op jit(solution)/shard_map/ppermute | solution.py:17
  356.5 8.8 %copy-start.23 = (pred[2,6]{1,0:T(4,128)(4,1)S(1)}, pred[2,6]{1,0:T(4,128)(4,1)}, u32[]{:S(2)}) copy-start(pred[2,6]{1,0:T(4,128)(4,1)} %copy-done.22) | copy-start | bytes 40
  356.6 5.3 %collective-permute-start.15 = (f32[3,1,2,6,2,16,128]{6,5,4,3,2,1,0:T(8,128)S(1)}, f32[3,1,2,6,2,16,128]{6,5,4,3,2,1,0:T(8,128)S(1)}, u32[]{:S(2)}, u32[]{:S(2)}) collective-permute-start(f32[3,1,2,6,2,16,128]{6,5,4,3,2,1,0:T(8,128)S(1)} %pad_maximum_fusion.9), channel_id=1, source_target_pairs={{1,0},{2,1},{3,2},{5,4},{6,5},{7,6},{9,8},{10,9},{11,10},{13,12},{... | collective-permute-start | bytes 1769480 | tf_op jit(solution)/shard_map/ppermute | solution.py:18
  357.9 5.4 %collective-permute-start.14 = (f32[3,1,2,6,2,16,128]{6,5,4,3,2,1,0:T(8,128)S(1)}, f32[3,1,2,6,2,16,128]{6,5,4,3,2,1,0:T(8,128)}, u32[]{:S(2)}, u32[]{:S(2)}) collective-permute-start(f32[3,1,2,6,2,16,128]{6,5,4,3,2,1,0:T(8,128)S(1)} %pad_maximum_fusion.9), channel_id=1, source_target_pairs={{0,1},{1,2},{2,3},{4,5},{5,6},{6,7},{8,9},{9,10},{10,11},{12,13},{... | collective-permute-start | bytes 1769480 | tf_op jit(solution)/shard_map/ppermute | solution.py:17
  (11 other events, 19.6 us)
where the time goes:
time: 423 us; the launch traced here: 421 us
  blocking collectives  235 us (56%)
  matrix products  61.2 us (14%)
  starting transfers between devices  43.5 us (10%)
  other arithmetic  33.8 us (8%)
  waiting for transfers between devices  24.1 us (6%)
  local copies, waits for them, and re-layouts  22.5 us (5%)
    psum x4, blocking collectives, body(): lax.psum((local_terms, local_inner(image_block, image_block)), ('slab', '...  193 us
    psum x1, blocking collectives, body(): lax.psum(local_inner(start, start), ('slab', 'sub')) / entry_count  42 us
    ppermute x8, starting transfers between devices, extended(): before = lax.ppermute(last, axis, up)  33.2 us
    ppermute x8, waiting for transfers between devices, extended(): before = lax.ppermute(last, axis, up)  18.7 us
    dot_general x12, matrix products, complex_apply(): jnp.einsum(layout, matrix_real, vec_real, preferred_element_type=jnp.floa...  12.9 us
    dot_general x12, matrix products, complex_apply(): jnp.einsum(layout, matrix_real, vec_imag, preferred_element_type=jnp.floa...  11.8 us
    another operation x15, other arithmetic, normalize(): low_factor = jnp.linalg.cholesky(gram_matrix)  10.7 us
    ppermute x8, starting transfers between devices, extended(): after = lax.ppermute(leading, axis, down)  10.3 us
  transfers between devices with their start and end apart: 16, of which 11 were waited for; matrix products, arithmetic and copies ran while one was open for 1% of the time, Pallas kernels for 0%

commit v1 on v0

--- a/solution.py
+++ b/solution.py
@@ -126,7 +126,9 @@
 def body(start, inv_factor, partner, partner_face, elem_class, elem_face, load_map, trace_map):
     rhs_count = start.shape[3]
     entry_count = start.size // rhs_count * lax.axis_size("slab") * lax.axis_size("sub")
-    start_gram = lax.psum(local_inner(start, start), ("slab", "sub")) / entry_count
+    start_gram = (
+        jnp.sum(lax.all_gather(local_inner(start, start), ("slab", "sub")), axis=0) / entry_count
+    )
     basis_block, upper_factor = normalize(start, start_gram)
     blocks = [basis_block]
     hessenberg = jnp.zeros((ITERS, ITERS + 1, rhs_count, rhs_count), jnp.float32)

time: 423 us -> 422 us (level)
    all_gather x0 -> x1, blocking collectives: none -> 44 us  [body(): lax.all_gather(local_inner(start, start), ('slab', 'sub'))]
    psum x1 -> x0, blocking collectives: 42 us -> none  [body(): lax.psum(local_inner(start, start), ('slab', 'sub')) / entry_count]
where the time goes in v1:
time: 422 us; the launch traced here: 421 us
  blocking collectives  234 us (55%)
  matrix products  61.1 us (14%)
  starting transfers between devices  43.3 us (10%)
  other arithmetic  33.8 us (8%)
  waiting for transfers between devices  24.5 us (6%)
  local copies, waits for them, and re-layouts  22.5 us (5%)
    psum x4, blocking collectives, body(): lax.psum((local_terms, local_inner(image_block, image_block)), ('slab', '...  190 us
    all_gather x1, blocking collectives, body(): lax.all_gather(local_inner(start, start), ('slab', 'sub'))  44 us
    ppermute x8, starting transfers between devices, extended(): before = lax.ppermute(last, axis, up)  32.9 us
    ppermute x8, waiting for transfers between devices, extended(): before = lax.ppermute(last, axis, up)  16.8 us
    dot_general x12, matrix products, complex_apply(): jnp.einsum(layout, matrix_real, vec_real, preferred_element_type=jnp.floa...  12.9 us
    dot_general x12, matrix products, complex_apply(): jnp.einsum(layout, matrix_real, vec_imag, preferred_element_type=jnp.floa...  11.8 us
    another operation x15, other arithmetic, normalize(): low_factor = jnp.linalg.cholesky(gram_matrix)  10.7 us
    ppermute x8, starting transfers between devices, extended(): after = lax.ppermute(leading, axis, down)  10.3 us
  transfers between devices with their start and end apart: 16, of which 11 were waited for; matrix products, arithmetic and copies ran while one was open for 1% of the time, Pallas kernels for 0%

profile of v1, /device:TPU:0, one launch (start us, length us, event | category | flops | bytes accessed | tf_op | source)
XLA Modules:
  0.0 421.0 jit_solution(3401171294624264121)
XLA Ops:
  2.8 2.1 gather_fusion
  7.2 44.0 %all-gather = f32[512,16]{1,0:T(8,128)S(1)} all-gather(f32[16,16]{1,0:T(8,128)S(1)} %convolution_bitcast_fusion.21), channel_id=2, replica_groups=mesh['slab'=8,'sub'=4] {'slab','sub'}, dimensions={0}, use_global_device_ids=true | all-gather | bytes 33792 | tf_op jit(solution)/shard_map/all_gather | solution.py:130
  57.4 2.0 fusion.119
  59.5 1.9 fusion.13
  61.3 1.9 fusion.12
  67.1 2.1 gather_fusion.1
  75.9 4.6 %collective-permute-start = (f32[1,1,2,6,2,16,128]{6,5,4,3,2,1,0:T(8,128)S(1)}, f32[1,1,2,6,2,16,128]{6,5,4,3,2,1,0:T(8,128)S(1)}, u32[]{:S(2)}, u32[]{:S(2)}) collective-permute-start(f32[1,1,2,6,2,16,128]{6,5,4,3,2,1,0:T(8,128)S(1)} %fusion.108), channel_id=1, source_target_pairs={{0,4},{4,8},{8,12},{12,16},{16,20},{20,24},{24,28},{1,5},{5,9},{9,... | collective-permute-start | bytes 589832 | tf_op jit(solution)/shard_map/ppermute | solution.py:17
  80.5 3.2 collective-permute-done.1
  87.0 3.9 collective-permute-start.2
  92.0 2.7 pad_maximum_fusion
  94.7 2.0 gather_fusion.2
  97.6 46.6 %all-reduce.4 = (f32[16,16]{0,1:T(8,128)S(1)}, f32[1,16,16]{2,1,0:T(8,128)S(1)}) all-reduce(f32[16,16]{0,1:T(8,128)S(1)} %convolution_bitcast_fusion.20, f32[1,16,16]{2,1,0:T(8,128)S(1)} %convolution_bitcast_fusion.19), channel_id=1, replica_groups=mesh['slab'=8,'sub'=4] {'slab','sub'}, use_global_device_ids=true, to_apply=%region_3.7 | all-reduce | flops 512 | bytes 4096 | tf_op jit(solution)/shard_map/psum | solution.py:150
  150.7 2.0 fusion.116
  152.7 1.9 fusion.117
  164.8 4.8 %collective-permute-start.4 = (f32[1,1,2,6,2,16,128]{6,5,4,3,2,1,0:T(8,128)S(1)}, f32[1,1,2,6,2,16,128]{6,5,4,3,2,1,0:T(8,128)S(1)}, u32[]{:S(2)}, u32[]{:S(2)}) collective-permute-start(f32[1,1,2,6,2,16,128]{6,5,4,3,2,1,0:T(8,128)S(1)} %fusion.103), channel_id=1, source_target_pairs={{0,4},{4,8},{8,12},{12,16},{16,20},{20,24},{24,28},{1,5},{5,9},{9,... | collective-permute-start | bytes 589832 | tf_op jit(solution)/shard_map/ppermute | solution.py:17
  169.7 2.6 collective-permute-done.5
  172.3 4.4 %collective-permute-done.4 = f32[1,1,2,6,2,16,128]{6,5,4,3,2,1,0:T(8,128)S(1)} collective-permute-done((f32[1,1,2,6,2,16,128]{6,5,4,3,2,1,0:T(8,128)S(1)}, f32[1,1,2,6,2,16,128]{6,5,4,3,2,1,0:T(8,128)S(1)}, u32[]{:S(2)}, u32[]{:S(2)}) %collective-permute-start.4) | collective-permute-done | bytes 196640 | tf_op jit(solution)/shard_map/ppermute | solution.py:17
  178.0 3.1 collective-permute-start.6
  184.0 2.0 gather_fusion.3
  187.0 47.7 %all-reduce.3 = (f32[2,16,16]{2,1,0:T(8,128)S(1)}, f32[16,16]{0,1:T(8,128)S(1)}) all-reduce(f32[2,16,16]{2,1,0:T(8,128)S(1)} %convolution_bitcast_fusion.7, f32[16,16]{0,1:T(8,128)S(1)} %convolution_bitcast_fusion.18), channel_id=1, replica_groups=mesh['slab'=8,'sub'=4] {'slab','sub'}, use_global_device_ids=true, to_apply=%region_6.10 | all-reduce | flops 768 | bytes 6144 | tf_op jit(solution)/shard_map/psum | solution.py:150
  241.3 2.0 fusion.114
  255.4 4.9 %collective-permute-start.8 = (f32[1,1,2,6,2,16,128]{6,5,4,3,2,1,0:T(8,128)S(1)}, f32[1,1,2,6,2,16,128]{6,5,4,3,2,1,0:T(8,128)S(1)}, u32[]{:S(2)}, u32[]{:S(2)}) collective-permute-start(f32[1,1,2,6,2,16,128]{6,5,4,3,2,1,0:T(8,128)S(1)} %fusion.101), channel_id=1, source_target_pairs={{0,4},{4,8},{8,12},{12,16},{16,20},{20,24},{24,28},{1,5},{5,9},{9,... | collective-permute-start | bytes 589832 | tf_op jit(solution)/shard_map/ppermute | solution.py:17
  261.9 3.9 collective-permute-done.8
  267.2 3.1 collective-permute-start.10
  273.3 2.0 gather_fusion.4
  276.4 49.0 %all-reduce.2 = (f32[3,16,16]{2,1,0:T(8,128)S(1)}, f32[16,16]{0,1:T(8,128)S(1)}) all-reduce(f32[3,16,16]{2,1,0:T(8,128)S(1)} %convolution_bitcast_fusion.6, f32[16,16]{0,1:T(8,128)S(1)} %convolution_bitcast_fusion.17), channel_id=1, replica_groups=mesh['slab'=8,'sub'=4] {'slab','sub'}, use_global_device_ids=true, to_apply=%region_8.12 | all-reduce | flops 1024 | bytes 8192 | tf_op jit(solution)/shard_map/psum | solution.py:150
  332.1 2.0 fusion.112
  334.1 1.9 fusion.113
  346.2 4.8 %collective-permute-start.12 = (f32[1,1,2,6,2,16,128]{6,5,4,3,2,1,0:T(8,128)S(1)}, f32[1,1,2,6,2,16,128]{6,5,4,3,2,1,0:T(8,128)S(1)}, u32[]{:S(2)}, u32[]{:S(2)}) collective-permute-start(f32[1,1,2,6,2,16,128]{6,5,4,3,2,1,0:T(8,128)S(1)} %fusion.99), channel_id=1, source_target_pairs={{0,4},{4,8},{8,12},{12,16},{16,20},{20,24},{24,28},{1,5},{5,9},{9,... | collective-permute-start | bytes 589832 | tf_op jit(solution)/shard_map/ppermute | solution.py:17
  352.8 3.8 collective-permute-done.12
  357.9 3.8 collective-permute-start.14
  366.6 47.0 %all-reduce.1 = (f32[4,16,16]{2,1,0:T(8,128)S(1)}, f32[16,16]{0,1:T(8,128)S(1)}) all-reduce(f32[4,16,16]{2,1,0:T(8,128)S(1)} %convolution_bitcast_fusion.5, f32[16,16]{0,1:T(8,128)S(1)} %convolution_bitcast_fusion.16), channel_id=1, replica_groups=mesh['slab'=8,'sub'=4] {'slab','sub'}, use_global_device_ids=true, to_apply=%region_10.14 | all-reduce | flops 1280 | bytes 10240 | tf_op jit(solution)/shard_map/psum | solution.py:150
  (253 shorter events, 105.9 us)
Async XLA Ops:
  6.9 49.9 %copy-start.2 = (bf16[32,2,128,128]{3,2,0,1:T(8,128)(2,1)}, bf16[32,2,128,128]{3,2,0,1:T(8,128)(2,1)S(1)}, u32[]{:S(2)}) copy-start(bf16[32,2,128,128]{3,2,0,1:T(8,128)(2,1)S(1)} %copy.73) | copy-start | bytes 6291460
  57.4 5.8 %copy-start.1 = (bf16[32,2,128,128]{3,2,1,0:T(8,128)(2,1)S(1)}, bf16[32,2,128,128]{3,2,1,0:T(8,128)(2,1)}, u32[]{:S(2)}) copy-start(bf16[32,2,128,128]{3,2,1,0:T(8,128)(2,1)} %param.34) | copy-start | bytes 6291460
  74.1 16.8 %copy-start.24 = (s32[2,6]{1,0:T(2,128)S(1)}, s32[2,6]{1,0:T(2,128)}, u32[]{:S(2)}) copy-start(s32[2,6]{1,0:T(2,128)} %param.36) | copy-start | bytes 148
  74.1 16.8 %copy-start.25 = (s32[2,6]{1,0:T(2,128)S(1)}, s32[2,6]{1,0:T(2,128)}, u32[]{:S(2)}) copy-start(s32[2,6]{1,0:T(2,128)} %param.35) | copy-start | bytes 148
  74.1 16.8 %copy-start.26 = (s32[6]{0:T(128)S(1)}, s32[6]{0:T(128)}, u32[]{:S(2)}) copy-start(s32[6]{0:T(128)} %constant.343) | copy-start | bytes 76
  74.6 9.0 %collective-permute-start.1 = (f32[1,1,2,6,2,16,128]{6,5,4,3,2,1,0:T(8,128)S(1)}, f32[1,1,2,6,2,16,128]{6,5,4,3,2,1,0:T(8,128)S(1)}, u32[]{:S(2)}, u32[]{:S(2)}) collective-permute-start(f32[1,1,2,6,2,16,128]{6,5,4,3,2,1,0:T(8,128)S(1)} %fusion.108), channel_id=1, source_target_pairs={{4,0},{8,4},{12,8},{16,12},{20,16},{24,20},{28,24},{5,1},{9,5},{13... | collective-permute-start | bytes 589832 | tf_op jit(solution)/shard_map/ppermute | solution.py:18
  75.9 8.9 %collective-permute-start = (f32[1,1,2,6,2,16,128]{6,5,4,3,2,1,0:T(8,128)S(1)}, f32[1,1,2,6,2,16,128]{6,5,4,3,2,1,0:T(8,128)S(1)}, u32[]{:S(2)}, u32[]{:S(2)}) collective-permute-start(f32[1,1,2,6,2,16,128]{6,5,4,3,2,1,0:T(8,128)S(1)} %fusion.108), channel_id=1, source_target_pairs={{0,4},{4,8},{8,12},{12,16},{16,20},{20,24},{24,28},{1,5},{5,9},{9,... | collective-permute-start | bytes 589832 | tf_op jit(solution)/shard_map/ppermute | solution.py:17
  85.7 5.3 %collective-permute-start.3 = (f32[3,1,2,6,2,16,128]{6,5,4,3,2,1,0:T(8,128)}, f32[3,1,2,6,2,16,128]{6,5,4,3,2,1,0:T(8,128)}, u32[]{:S(2)}, u32[]{:S(2)}) collective-permute-start(f32[3,1,2,6,2,16,128]{6,5,4,3,2,1,0:T(8,128)} %pad_maximum_fusion.5), channel_id=1, source_target_pairs={{1,0},{2,1},{3,2},{5,4},{6,5},{7,6},{9,8},{10,9},{11,10},{13,12},{... | collective-permute-start | bytes 1769480 | tf_op jit(solution)/shard_map/ppermute | solution.py:18
  87.0 5.0 %collective-permute-start.2 = (f32[3,1,2,6,2,16,128]{6,5,4,3,2,1,0:T(8,128)}, f32[3,1,2,6,2,16,128]{6,5,4,3,2,1,0:T(8,128)}, u32[]{:S(2)}, u32[]{:S(2)}) collective-permute-start(f32[3,1,2,6,2,16,128]{6,5,4,3,2,1,0:T(8,128)} %pad_maximum_fusion.5), channel_id=1, source_target_pairs={{0,1},{1,2},{2,3},{4,5},{5,6},{6,7},{8,9},{9,10},{10,11},{12,13},{... | collective-permute-start | bytes 1769480 | tf_op jit(solution)/shard_map/ppermute | solution.py:17
  91.0 184.3 %copy-start.22 = (pred[2,6]{1,0:T(4,128)(4,1)}, pred[2,6]{1,0:T(4,128)(4,1)S(1)}, u32[]{:S(2)}) copy-start(pred[2,6]{1,0:T(4,128)(4,1)S(1)} %broadcast_compare_fusion) | copy-start | bytes 40
  150.6 4.0 copy-start.3
  163.5 8.7 %collective-permute-start.5 = (f32[1,1,2,6,2,16,128]{6,5,4,3,2,1,0:T(8,128)S(1)}, f32[1,1,2,6,2,16,128]{6,5,4,3,2,1,0:T(8,128)S(1)}, u32[]{:S(2)}, u32[]{:S(2)}) collective-permute-start(f32[1,1,2,6,2,16,128]{6,5,4,3,2,1,0:T(8,128)S(1)} %fusion.103), channel_id=1, source_target_pairs={{4,0},{8,4},{12,8},{16,12},{20,16},{24,20},{28,24},{5,1},{9,5},{13... | collective-permute-start | bytes 589832 | tf_op jit(solution)/shard_map/ppermute | solution.py:18
  164.8 11.8 %collective-permute-start.4 = (f32[1,1,2,6,2,16,128]{6,5,4,3,2,1,0:T(8,128)S(1)}, f32[1,1,2,6,2,16,128]{6,5,4,3,2,1,0:T(8,128)S(1)}, u32[]{:S(2)}, u32[]{:S(2)}) collective-permute-start(f32[1,1,2,6,2,16,128]{6,5,4,3,2,1,0:T(8,128)S(1)} %fusion.103), channel_id=1, source_target_pairs={{0,4},{4,8},{8,12},{12,16},{16,20},{20,24},{24,28},{1,5},{5,9},{9,... | collective-permute-start | bytes 589832 | tf_op jit(solution)/shard_map/ppermute | solution.py:17
  176.7 4.4 %collective-permute-start.7 = (f32[3,1,2,6,2,16,128]{6,5,4,3,2,1,0:T(8,128)S(1)}, f32[3,1,2,6,2,16,128]{6,5,4,3,2,1,0:T(8,128)S(1)}, u32[]{:S(2)}, u32[]{:S(2)}) collective-permute-start(f32[3,1,2,6,2,16,128]{6,5,4,3,2,1,0:T(8,128)S(1)} %pad_maximum_fusion.6), channel_id=1, source_target_pairs={{1,0},{2,1},{3,2},{5,4},{6,5},{7,6},{9,8},{10,9},{11,10},{13,12},{... | collective-permute-start | bytes 1769480 | tf_op jit(solution)/shard_map/ppermute | solution.py:18
  178.0 4.7 %collective-permute-start.6 = (f32[3,1,2,6,2,16,128]{6,5,4,3,2,1,0:T(8,128)S(1)}, f32[3,1,2,6,2,16,128]{6,5,4,3,2,1,0:T(8,128)S(1)}, u32[]{:S(2)}, u32[]{:S(2)}) collective-permute-start(f32[3,1,2,6,2,16,128]{6,5,4,3,2,1,0:T(8,128)S(1)} %pad_maximum_fusion.6), channel_id=1, source_target_pairs={{0,1},{1,2},{2,3},{4,5},{5,6},{6,7},{8,9},{9,10},{10,11},{12,13},{... | collective-permute-start | bytes 1769480 | tf_op jit(solution)/shard_map/ppermute | solution.py:17
  234.7 5.3 %copy-start.16 = (f32[2,16,16]{2,1,0:T(8,128)}, f32[2,16,16]{2,1,0:T(8,128)S(1)}, u32[]{:S(2)}) copy-start(f32[2,16,16]{2,1,0:T(8,128)S(1)} %get-tuple-element.105) | copy-start | bytes 6148
  241.2 4.0 copy-start.4
  254.1 7.9 %collective-permute-start.9 = (f32[1,1,2,6,2,16,128]{6,5,4,3,2,1,0:T(8,128)S(1)}, f32[1,1,2,6,2,16,128]{6,5,4,3,2,1,0:T(8,128)S(1)}, u32[]{:S(2)}, u32[]{:S(2)}) collective-permute-start(f32[1,1,2,6,2,16,128]{6,5,4,3,2,1,0:T(8,128)S(1)} %fusion.101), channel_id=1, source_target_pairs={{4,0},{8,4},{12,8},{16,12},{20,16},{24,20},{28,24},{5,1},{9,5},{13... | collective-permute-start | bytes 589832 | tf_op jit(solution)/shard_map/ppermute | solution.py:18
  255.4 10.5 %collective-permute-start.8 = (f32[1,1,2,6,2,16,128]{6,5,4,3,2,1,0:T(8,128)S(1)}, f32[1,1,2,6,2,16,128]{6,5,4,3,2,1,0:T(8,128)S(1)}, u32[]{:S(2)}, u32[]{:S(2)}) collective-permute-start(f32[1,1,2,6,2,16,128]{6,5,4,3,2,1,0:T(8,128)S(1)} %fusion.101), channel_id=1, source_target_pairs={{0,4},{4,8},{8,12},{12,16},{16,20},{20,24},{24,28},{1,5},{5,9},{9,... | collective-permute-start | bytes 589832 | tf_op jit(solution)/shard_map/ppermute | solution.py:17
  265.9 5.0 %collective-permute-start.11 = (f32[3,1,2,6,2,16,128]{6,5,4,3,2,1,0:T(8,128)S(1)}, f32[3,1,2,6,2,16,128]{6,5,4,3,2,1,0:T(8,128)S(1)}, u32[]{:S(2)}, u32[]{:S(2)}) collective-permute-start(f32[3,1,2,6,2,16,128]{6,5,4,3,2,1,0:T(8,128)S(1)} %pad_maximum_fusion.7), channel_id=1, source_target_pairs={{1,0},{2,1},{3,2},{5,4},{6,5},{7,6},{9,8},{10,9},{11,10},{13,12},{... | collective-permute-start | bytes 1769480 | tf_op jit(solution)/shard_map/ppermute | solution.py:18
  267.2 4.7 %collective-permute-start.10 = (f32[3,1,2,6,2,16,128]{6,5,4,3,2,1,0:T(8,128)S(1)}, f32[3,1,2,6,2,16,128]{6,5,4,3,2,1,0:T(8,128)S(1)}, u32[]{:S(2)}, u32[]{:S(2)}) collective-permute-start(f32[3,1,2,6,2,16,128]{6,5,4,3,2,1,0:T(8,128)S(1)} %pad_maximum_fusion.7), channel_id=1, source_target_pairs={{0,1},{1,2},{2,3},{4,5},{5,6},{6,7},{8,9},{9,10},{10,11},{12,13},{... | collective-permute-start | bytes 1769480 | tf_op jit(solution)/shard_map/ppermute | solution.py:17
  325.4 5.4 %copy-start.14 = (f32[3,16,16]{2,1,0:T(8,128)}, f32[3,16,16]{2,1,0:T(8,128)S(1)}, u32[]{:S(2)}) copy-start(f32[3,16,16]{2,1,0:T(8,128)S(1)} %get-tuple-element.103) | copy-start | bytes 9220
  343.7 7.4 %copy-start.18 = (f32[1,1,16,16]{2,3,1,0:T(8,128)S(1)}, f32[1,1,16,16]{2,3,1,0:T(8,128)}, u32[]{:S(2)}) copy-start(f32[1,1,16,16]{2,3,1,0:T(8,128)} %get-tuple-element.115) | copy-start | bytes 3076
  343.7 8.7 %copy-start.19 = (f32[1,1,16,16]{2,3,1,0:T(8,128)S(1)}, f32[1,1,16,16]{2,3,1,0:T(8,128)}, u32[]{:S(2)}) copy-start(f32[1,1,16,16]{2,3,1,0:T(8,128)} %get-tuple-element.113) | copy-start | bytes 3076
  344.4 17.4 %copy-start.17 = (f32[2,16,16]{2,1,0:T(8,128)S(1)}, f32[2,16,16]{2,1,0:T(8,128)}, u32[]{:S(2)}) copy-start(f32[2,16,16]{2,1,0:T(8,128)} %copy-done.16) | copy-start | bytes 6148
  344.4 17.4 %copy-start.20 = (f32[1,1,16,16]{2,3,1,0:T(8,128)S(1)}, f32[1,1,16,16]{2,3,1,0:T(8,128)}, u32[]{:S(2)}) copy-start(f32[1,1,16,16]{2,3,1,0:T(8,128)} %get-tuple-element.111) | copy-start | bytes 3076
  344.4 17.5 %copy-start.15 = (f32[3,16,16]{2,1,0:T(8,128)S(1)}, f32[3,16,16]{2,1,0:T(8,128)}, u32[]{:S(2)}) copy-start(f32[3,16,16]{2,1,0:T(8,128)} %copy-done.14) | copy-start | bytes 9220
  344.9 7.8 %collective-permute-start.13 = (f32[1,1,2,6,2,16,128]{6,5,4,3,2,1,0:T(8,128)S(1)}, f32[1,1,2,6,2,16,128]{6,5,4,3,2,1,0:T(8,128)S(1)}, u32[]{:S(2)}, u32[]{:S(2)}) collective-permute-start(f32[1,1,2,6,2,16,128]{6,5,4,3,2,1,0:T(8,128)S(1)} %fusion.99), channel_id=1, source_target_pairs={{4,0},{8,4},{12,8},{16,12},{20,16},{24,20},{28,24},{5,1},{9,5},{13... | collective-permute-start | bytes 589832 | tf_op jit(solution)/shard_map/ppermute | solution.py:18
  346.2 10.3 %collective-permute-start.12 = (f32[1,1,2,6,2,16,128]{6,5,4,3,2,1,0:T(8,128)S(1)}, f32[1,1,2,6,2,16,128]{6,5,4,3,2,1,0:T(8,128)S(1)}, u32[]{:S(2)}, u32[]{:S(2)}) collective-permute-start(f32[1,1,2,6,2,16,128]{6,5,4,3,2,1,0:T(8,128)S(1)} %fusion.99), channel_id=1, source_target_pairs={{0,4},{4,8},{8,12},{12,16},{16,20},{20,24},{24,28},{1,5},{5,9},{9,... | collective-permute-start | bytes 589832 | tf_op jit(solution)/shard_map/ppermute | solution.py:17
  356.6 8.8 %copy-start.23 = (pred[2,6]{1,0:T(4,128)(4,1)S(1)}, pred[2,6]{1,0:T(4,128)(4,1)}, u32[]{:S(2)}) copy-start(pred[2,6]{1,0:T(4,128)(4,1)} %copy-done.22) | copy-start | bytes 40
  356.6 5.3 %collective-permute-start.15 = (f32[3,1,2,6,2,16,128]{6,5,4,3,2,1,0:T(8,128)S(1)}, f32[3,1,2,6,2,16,128]{6,5,4,3,2,1,0:T(8,128)S(1)}, u32[]{:S(2)}, u32[]{:S(2)}) collective-permute-start(f32[3,1,2,6,2,16,128]{6,5,4,3,2,1,0:T(8,128)S(1)} %pad_maximum_fusion.9), channel_id=1, source_target_pairs={{1,0},{2,1},{3,2},{5,4},{6,5},{7,6},{9,8},{10,9},{11,10},{13,12},{... | collective-permute-start | bytes 1769480 | tf_op jit(solution)/shard_map/ppermute | solution.py:18
  357.9 5.4 %collective-permute-start.14 = (f32[3,1,2,6,2,16,128]{6,5,4,3,2,1,0:T(8,128)S(1)}, f32[3,1,2,6,2,16,128]{6,5,4,3,2,1,0:T(8,128)}, u32[]{:S(2)}, u32[]{:S(2)}) collective-permute-start(f32[3,1,2,6,2,16,128]{6,5,4,3,2,1,0:T(8,128)S(1)} %pad_maximum_fusion.9), channel_id=1, source_target_pairs={{0,1},{1,2},{2,3},{4,5},{5,6},{6,7},{8,9},{9,10},{10,11},{12,13},{... | collective-permute-start | bytes 1769480 | tf_op jit(solution)/shard_map/ppermute | solution.py:17
  (11 other events, 19.6 us)
